TPU v7x, 32 devices: a whole 2x2x4 slice. The times are simulated.
32 devices in a mesh: sector: 16 (over z, y, x), dof: 2 (over core).
Axes of the slice: x: 2, y: 2, z: 4, core: 2. Of those that a mesh axis runs over, the one named last changes fastest.
Arguments:
- loads: bfloat16 [16, 128, 32768], P('sector', None, 'dof'), may hold values from -0.75 to 0.75
- modes: bfloat16 [32768, 512], P('dof'), may hold values from -0.25 to 0.25
- response: float32 [16, 128, 512], P('sector', None, 'dof'), may hold values from -6 to 6
- pattern: int32 [16], P('sector'), may hold values from 0 to 7
- deviation: float32 [8, 512], replicated, may hold values from -1 to 1
- eigen: float32 [16, 512], replicated, may hold values from 1 to 10
- loss: float32 [512], replicated, may hold values from 0.2 to 0.6
- omega_sq: float32 [64], replicated, may hold values from 0.5 to 12
- iface_left: int32 [1024], P('dof'), may hold values from 0 to 16383, as said below
- iface_right: int32 [1024], P('dof'), may hold values from 0 to 16383, as said below
Outputs:
- modal_response: float32 [16, 128, 512], P('sector', None, 'dof')
- displacement: bfloat16 [16, 128, 32768], P('sector', None, 'dof')
Inputs may be any that keep to these rules, and one draw needn't show every extreme that they name: Within each block of 512 entries, the entries of iface_left and of iface_right together are (2) * 512 distinct rows. `iface_right`: see iface_left.
All inputs are finite; a program needn't handle non-finite values.
Results may differ from a plain program's by a relative error of at most 0.005.
Values may be sent and summed in bfloat16 or wider, within the bound.
A program may use at most 128 MiB of HBM per device.

v0:
```python
import math
import jax
import jax.numpy as jnp
from jax import lax
from jax.sharding import PartitionSpec as P


def shifted_2(shard, axis, by):
    size = lax.axis_size(axis)
    return lax.ppermute(shard, axis, [(i, (i + by) % size) for i in range(size)])


def tables(row_count, col_count, sectors):
    rows_idx = jnp.arange(row_count, dtype=jnp.int32) % sectors
    cols_idx = jnp.arange(col_count, dtype=jnp.int32) % sectors
    turns = rows_idx[:, None] * cols_idx[None, :] % sectors
    theta = turns.astype(jnp.float32) * (2.0 * math.pi / sectors)
    return (jnp.cos(theta), jnp.sin(theta))


def divide(spec_re, spec_im, shifted, damped):
    denom = shifted * shifted + damped * damped
    return (
        (spec_re * shifted + spec_im * damped) / denom,
        (spec_im * shifted - spec_re * damped) / denom,
    )


def shards(
    loads, modes, response, pattern, deviation, eigen, loss, omega_sq, iface_left, iface_right
):
    highest = lax.Precision.HIGHEST
    local_sec, rows_two, dof_rows = loads.shape
    freqs = rows_two // 2
    modes_all = modes.shape[1]
    sec_devices = lax.axis_size("sector")
    sectors = sec_devices * local_sec
    half = modes_all // lax.axis_size("dof")
    width = freqs * half
    first_mode = lax.axis_index("dof") * half
    partial_force = jnp.dot(
        loads.reshape(local_sec * rows_two, dof_rows), modes, preferred_element_type=jnp.float32
    )
    force = lax.psum_scatter(
        partial_force.reshape(local_sec, rows_two, modes_all),
        "dof",
        scatter_dimension=2,
        tiled=True,
    )
    table_count = deviation.shape[0]
    dev_half = lax.dynamic_slice_in_dim(deviation, first_mode, half, 1)
    onehot = (pattern[:, None] == jnp.arange(table_count, dtype=jnp.int32)[None, :]).astype(
        jnp.float32
    )
    dev_rows = jnp.dot(onehot, dev_half, precision=highest)
    rest = (force - dev_rows[:, None, :] * response).reshape(local_sec, 2, width)
    columns = lax.all_to_all(rest, "sector", split_axis=2, concat_axis=0, tiled=True)
    share = width // sec_devices
    col_idx = lax.axis_index("sector") * share + jnp.arange(share, dtype=jnp.int32)
    freq_idx = col_idx // half
    mode_idx = first_mode + col_idx % half
    stiff = jnp.take(eigen, mode_idx, axis=1)
    shifted = stiff - jnp.take(omega_sq, freq_idx)[None, :]
    damped = jnp.take(loss, mode_idx)[None, :] * stiff
    cosine, sine = tables(sectors, sectors, sectors)
    spec_re = jnp.dot(cosine, columns[:, 0], precision=highest) + jnp.dot(
        sine, columns[:, 1], precision=highest
    )
    spec_im = jnp.dot(cosine, columns[:, 1], precision=highest) - jnp.dot(
        sine, columns[:, 0], precision=highest
    )
    solved_re, solved_im = divide(spec_re, spec_im, shifted, damped)
    out_re = (
        jnp.dot(cosine, solved_re, precision=highest) - jnp.dot(sine, solved_im, precision=highest)
    ) / sectors
    out_im = (
        jnp.dot(cosine, solved_im, precision=highest) + jnp.dot(sine, solved_re, precision=highest)
    ) / sectors
    updated = lax.all_to_all(
        jnp.stack([out_re, out_im], 1).astype(jnp.bfloat16),
        "sector",
        split_axis=0,
        concat_axis=2,
        tiled=True,
    ).astype(jnp.float32)
    modal_response = updated.reshape(local_sec, rows_two, half)
    rounded = modal_response.astype(jnp.bfloat16)
    raw = jnp.einsum(
        "skm,dm->skd",
        lax.all_gather(rounded, "dof", axis=2, tiled=True),
        modes,
        preferred_element_type=jnp.float32,
    ).astype(jnp.bfloat16)
    left_vals = jnp.take(raw, iface_left, axis=2)
    right_vals = jnp.take(raw, iface_right, axis=2)
    next_left = shifted_2(left_vals, "sector", -1)
    prev_right = shifted_2(right_vals, "sector", 1)
    left_after = jnp.concatenate([left_vals[1:], next_left], 0)
    right_before = jnp.concatenate([prev_right, right_vals[:-1]], 0)
    right_new = (0.5 * (right_vals.astype(jnp.float32) + left_after.astype(jnp.float32))).astype(
        jnp.bfloat16
    )
    left_new = (0.5 * (right_before.astype(jnp.float32) + left_vals.astype(jnp.float32))).astype(
        jnp.bfloat16
    )
    displacement = raw.at[:, :, iface_right].set(right_new).at[:, :, iface_left].set(left_new)
    return (modal_response, displacement)


def solution(mesh):
    placed = (
        P("sector", None, "dof"),
        P("dof", None),
        P("sector", None, "dof"),
        P("sector"),
        P(),
        P(),
        P(),
        P(),
        P("dof"),
        P("dof"),
    )
    return jax.shard_map(
        shards,
        mesh=mesh,
        in_specs=placed,
        out_specs=(P("sector", None, "dof"), P("sector", None, "dof")),
        check_vma=False,
    )
```

profile of v0, /device:TPU:0, one launch (start us, length us, event | category | flops | bytes accessed | tf_op | source)
XLA Modules:
  0.0 273.0 jit_solution(13463132247253687220)
XLA Ops:
  7.3 10.1 %fusion.2 = f32[1,128,512]{2,1,0:T(8,128)} fusion(bf16[16384,512]{1,0:T(8,128)(2,1)} %param.13, bf16[1,128,16384]{2,1,0:T(8,128)(2,1)} %param.12), kind=kOutput, calls=%fused_computation.9 | convolution fusion | flops 2147483648 | bytes 21233664 | tf_op jit(solution)/shard_map/dot_general | solution.py:41
  19.0 0.7 fusion.90
  19.8 0.7 fusion.91
  20.4 0.7 fusion.88
  21.2 0.7 fusion.89
  22.7 6.9 %gather_fusion.1 = f32[1024]{0:T(1024)S(1)} fusion(f32[512]{0:T(512)S(1)} %copy-done.1, s32[1024]{0:T(1024)S(1)} %broadcast_clamp_fusion), kind=kCustom, calls=%fused_computation.3 | custom fusion | bytes 12288 | tf_op jit(solution)/shard_map/jit(_take)/gather | solution.py:64
  29.5 0.1 fusion.30
  29.7 4.4 %compare_select_fusion.2 = f32[1024,1]{0,1:T(1,128)S(1)} fusion(f32[]{:T(128)} %bitcast.69, f32[]{:T(128)} %bitcast.70, f32[]{:T(128)} %bitcast.71, f32[]{:T(128)} %bitcast.72, f32[]{:T(128)} %bitcast.73, f32[]{:T(128)} %bitcast.75, f32[]{:T(128)} %bitcast.74, s32[]{:T(128)S(6)} %mul.129), kind=kLoop, calls=%fused_computation.107 | loop fusion | flops 31744 | bytes 4128 | tf_op jit(solution)/shard_map/jit(_take)/gather | solution.py:63
  34.1 0.9 multiply_subtract_fusion
  35.0 0.1 reshape.256
  35.1 12.0 %copy.32 = f32[1,2,16384]{1,0,2:T(1,128)} copy(f32[1,2,16384]{2,1,0:T(2,128)S(1)} %reshape.256) | data formatting | bytes 262144 | tf_op jit(solution)/shard_map/reshape | solution.py:56
  47.2 0.5 broadcast.1041
  47.7 74.5 %reduce.114 = f32[16384,2]{1,0:T(8,128)} reduce(f32[16384,1,2]{2,1,0:T(1,128)} %bitcast.171, f32[]{:T(128)} %broadcast.1041), dimensions={1}, to_apply=%bitcast.154.reduce_sub_computation | reduce | bytes 262148
  122.1 8.2 %reshape.603 = f32[16,1,2048]{2,1,0:T(1,128)} reshape(f32[16384,2]{1,0:T(8,128)} %reduce.114) | data formatting | bytes 262144
  130.4 8.4 %all-to-all-start = ((f32[16,1,2048]{2,1,0:T(1,128)}), f32[16,1,2048]{2,1,0:T(1,128)S(1)}, u32[]{:S(2)}, u32[]{:S(2)}) async-start(f32[16,1,2048]{2,1,0:T(1,128)} %reshape.603), calls=%async_computation.1 | async-start | bytes 262144 | tf_op jit(solution)/shard_map/all_to_all | solution.py:57
  138.8 0.1 copy.34
  138.9 2.8 %gather_fusion = f32[1024,16]{1,0:T(8,128)S(1)} fusion(f32[16,512]{0,1:T(8,128)S(1)} %copy.34, s32[1024]{0:T(1024)S(1)} %broadcast_clamp_fusion), kind=kCustom, calls=%fused_computation.2 | custom fusion | bytes 135168 | tf_op jit(solution)/shard_map/jit(_take)/gather | solution.py:62
  141.7 0.2 copy.35
  141.9 0.1 compare_reduce_fusion.52
  142.0 35.5 %select_select_fusion = f32[1024]{0:T(1024)S(1)} fusion(pred[1024]{0:T(1024)(128)(4,1)S(1)} %get-tuple-element.77, pred[1024]{0:T(1024)(128)(4,1)S(1)} %get-tuple-element.78, pred[1024]{0:T(1024)(128)(4,1)S(1)} %get-tuple-element.79, pred[1024]{0:T(1024)(128)(4,1)S(1)} %get-tuple-element.80, pred[1024]{0:T(1024)(128)(4,1)S(1)} %get-tuple-element.81, ...), kind=kLoop, calls=%fused_computation.141 | loop fusion | flops 81920 | bytes 66792 | tf_op jit(solution)/shard_map/jit(_take)/select_n | solution.py:63
  177.6 1.0 reduce.115
  178.5 14.7 %reshape.604 = f32[16384,1,2]{2,1,0:T(1,128)} reshape(f32[16,2048]{1,0:T(8,128)S(1)} %reduce.115) | data formatting | bytes 262144
  193.3 5.2 %copy.42 = f32[1,2,16,1024]{3,2,1,0:T(8,128)S(1)} copy(f32[1,2,16,1024]{1,3,2,0:T(8,128)} %bitcast.172) | data formatting | bytes 262144 | tf_op jit(solution)/shard_map/all_to_all | solution.py:57
  198.5 0.3 fusion.25
  198.8 0.3 fusion.26
  199.1 0.3 convolution_add_fusion.1
  199.5 0.3 fusion.21
  199.8 0.3 fusion.39
  200.1 0.3 fusion.41
  200.4 0.3 fusion.9
  200.8 0.3 fusion.10
  201.1 0.7 copy.36
  201.8 6.9 %all-to-all-start.1 = ((bf16[16,2,1024]{2,1,0:T(2,128)(2,1)}), bf16[16,2,1024]{2,1,0:T(2,128)(2,1)S(1)}, u32[]{:S(2)}, u32[]{:S(2)}) async-start(bf16[16,2,1024]{2,1,0:T(2,128)(2,1)} %copy.36), calls=%async_computation.2 | async-start | bytes 131072 | tf_op jit(solution)/shard_map/all_to_all | solution.py:79
  208.7 7.5 %all-to-all-done.1 = bf16[16,2,1024]{2,1,0:T(2,128)(2,1)S(1)} async-done(((bf16[16,2,1024]{2,1,0:T(2,128)(2,1)}), bf16[16,2,1024]{2,1,0:T(2,128)(2,1)S(1)}, u32[]{:S(2)}, u32[]{:S(2)}) %all-to-all-start.1) | async-done | bytes 65568 | tf_op jit(solution)/shard_map/all_to_all | solution.py:79
  216.3 1.9 all_gather.3
  218.2 10.3 %convolution_convert_fusion = bf16[128,16384]{1,0:T(8,128)(2,1)} fusion(bf16[16384,512]{1,0:T(8,128)(2,1)} %param.13, bf16[1,128,512]{2,1,0:T(8,128)(2,1)S(1)} %all_gather.3), kind=kOutput, calls=%fused_computation.6 | convolution fusion | flops 2149580800 | bytes 21102592 | tf_op jit(solution)/shard_map/skm,dm->skd/dot_general | solution.py:88
  228.6 6.4 %copy.40 = bf16[128,16384]{0,1:T(8,128)(2,1)} copy(bf16[128,16384]{1,0:T(8,128)(2,1)} %convolution_convert_fusion) | data formatting | bytes 8388608 | tf_op jit(solution)/shard_map/convert_element_type | solution.py:93
  235.0 3.8 %gather_fusion.3 = bf16[512,128]{1,0:T(8,128)(2,1)S(1)} fusion(bf16[128,16384]{0,1:T(8,128)(2,1)} %copy.40, s32[1024]{0:T(1024)S(1)} %pad_clamp_fusion), kind=kCustom, calls=%fused_computation.1.clone | custom fusion | bytes 264192 | tf_op jit(solution)/shard_map/jit(_take)/gather | solution.py:94
  238.7 0.1 bitcast_select_fusion
  238.9 1.0 collective-permute-start
  239.9 3.8 %gather_fusion.2 = bf16[512,128]{1,0:T(8,128)(2,1)S(1)} fusion(bf16[128,16384]{0,1:T(8,128)(2,1)} %copy.40, s32[1024]{0:T(1024)S(1)} %pad_clamp_fusion.1), kind=kCustom, calls=%fused_computation.clone | custom fusion | bytes 264192 | tf_op jit(solution)/shard_map/jit(_take)/gather | solution.py:95
  243.7 0.1 bitcast_select_fusion.1
  243.8 1.3 collective-permute-start.1
  245.2 0.7 convert_element_type.61
  245.8 6.8 %scatter_custom_fusion = bf16[128,16384]{0,1:T(8,128)(2,1)} fusion(bf16[128,16384]{0,1:T(8,128)(2,1)} %copy.40, s32[512]{0:T(512)S(1)} %compare_select_fusion.14, bf16[1,128,512]{1,2,0:T(8,128)(2,1)S(1)} %collective-permute-done, f32[]{:T(128)} %constant.134.clone.1, bf16[512,128]{1,0:T(8,128)(2,1)S(1)} %gather_fusion.2, ...), kind=kCustom, calls=%fused_computation.23 | custom fusion | flops 393216 | bytes 4457472 | tf_op jit(solution)/shard_map/scatter | solution.py:106
  252.7 0.3 collective-permute-done.1
  253.0 6.8 %scatter_custom_fusion.1 = bf16[128,16384]{0,1:T(8,128)(2,1)} fusion(bf16[128,16384]{0,1:T(8,128)(2,1)} %scatter_custom_fusion, s32[512]{0:T(512)S(1)} %compare_select_fusion.13, bf16[1,128,512]{1,2,0:T(8,128)(2,1)S(1)} %collective-permute-done.1, f32[]{:T(128)} %constant.134.clone.1, bf16[512,128]{1,0:T(8,128)(2,1)S(1)} %gather_fusion.3, ...), kind=kCustom, calls=%fused_computation.25 | custom fusion | flops 393216 | bytes 4457472 | tf_op jit(solution)/shard_map/scatter | solution.py:106
  259.8 6.4 %copy.41 = bf16[1,128,16384]{2,1,0:T(8,128)(2,1)} copy(bf16[1,128,16384]{1,2,0:T(8,128)(2,1)} %bitcast.173) | data formatting | bytes 8388608
  (61 shorter events, 2.0 us)
Async XLA Ops:
  7.2 22.4 %copy-start = (f32[8,512]{1,0:T(8,128)S(1)}, f32[8,512]{1,0:T(8,128)}, u32[]{:S(2)}) copy-start(f32[8,512]{1,0:T(8,128)} %param.16) | copy-start | bytes 49156
  7.2 11.8 %copy-start.2 = (f32[64]{0:T(128)S(1)}, f32[64]{0:T(128)}, u32[]{:S(2)}) copy-start(f32[64]{0:T(128)} %param.19) | copy-start | bytes 772
  7.2 14.7 %copy-start.5 = (s32[512]{0:T(512)S(1)}, s32[512]{0:T(512)}, u32[]{:S(2)}) copy-start(s32[512]{0:T(512)} %param.21) | copy-start | bytes 6148
  7.2 15.4 %copy-start.6 = (s32[512]{0:T(512)S(1)}, s32[512]{0:T(512)}, u32[]{:S(2)}) copy-start(s32[512]{0:T(512)} %param.20) | copy-start | bytes 6148
  7.2 15.4 %copy-start.1 = (f32[512]{0:T(512)S(1)}, f32[512]{0:T(512)}, u32[]{:S(2)}) copy-start(f32[512]{0:T(512)} %param.18) | copy-start | bytes 6148
  7.2 26.9 %reduce-scatter.2.cloned.1.call-start = ((), (), s32[]{:S(2)}) async-start(), calls=%async_computation.3 | async-start | bytes 393216 | tf_op jit(solution)/shard_map/reduce_scatter | solution.py:44
  17.4 16.8 %copy-start.3 = (f32[1,128,256]{2,1,0:T(8,128)S(1)}, f32[1,128,256]{2,1,0:T(8,128)}, u32[]{:S(2)}) copy-start(f32[1,128,256]{2,1,0:T(8,128)} %param.14) | copy-start | bytes 393220
  122.1 16.6 %copy-start.4 = (f32[16,512]{1,0:T(8,128)S(1)}, f32[16,512]{1,0:T(8,128)}, u32[]{:S(2)}) copy-start(f32[16,512]{1,0:T(8,128)} %param.17) | copy-start | bytes 98308
  130.4 47.2 %all-to-all-start = ((f32[16,1,2048]{2,1,0:T(1,128)}), f32[16,1,2048]{2,1,0:T(1,128)S(1)}, u32[]{:S(2)}, u32[]{:S(2)}) async-start(f32[16,1,2048]{2,1,0:T(1,128)} %reshape.603), calls=%async_computation.1 | async-start | bytes 262144 | tf_op jit(solution)/shard_map/all_to_all | solution.py:57
  201.8 14.4 %all-to-all-start.1 = ((bf16[16,2,1024]{2,1,0:T(2,128)(2,1)}), bf16[16,2,1024]{2,1,0:T(2,128)(2,1)S(1)}, u32[]{:S(2)}, u32[]{:S(2)}) async-start(bf16[16,2,1024]{2,1,0:T(2,128)(2,1)} %copy.36), calls=%async_computation.2 | async-start | bytes 131072 | tf_op jit(solution)/shard_map/all_to_all | solution.py:79
  238.9 7.0 %collective-permute-start = (bf16[1,128,512]{1,2,0:T(8,128)(2,1)S(1)}, bf16[1,128,512]{1,2,0:T(8,128)(2,1)S(1)}, u32[]{:S(2)}, u32[]{:S(2)}) collective-permute-start(bf16[1,128,512]{1,2,0:T(8,128)(2,1)S(1)} %bitcast_select_fusion), channel_id=1, source_target_pairs={{0,30},{2,0},{4,2},{6,4},{8,6},{10,8},{12,10},{14,12},{16,14},{18,... | collective-permute-start | bytes 393224 | tf_op jit(solution)/shard_map/ppermute | solution.py:10
  243.8 9.1 %collective-permute-start.1 = (bf16[1,128,512]{1,2,0:T(8,128)(2,1)S(1)}, bf16[1,128,512]{1,2,0:T(8,128)(2,1)S(1)}, u32[]{:S(2)}, u32[]{:S(2)}) collective-permute-start(bf16[1,128,512]{1,2,0:T(8,128)(2,1)S(1)} %bitcast_select_fusion.1), channel_id=1, source_target_pairs={{0,2},{2,4},{4,6},{6,8},{8,10},{10,12},{12,14},{14,16},{16,18},{18... | collective-permute-start | bytes 393224 | tf_op jit(solution)/shard_map/ppermute | solution.py:10
Sparse Core Ops, SparseCore 0:
  17.5 10.4 reduce-scatter.1
where the time goes:
time: 274 us; the launch traced here: 273 us
  other arithmetic  133 us (49%)
  local copies, waits for them, and re-layouts  74.7 us (27%)
  matrix products  23.1 us (8%)
  starting transfers between devices  17.6 us (6%)
  between operations  15.1 us (6%)
  waiting for transfers between devices  7.82 us (3%)
    unnamed x1, other arithmetic  74.5 us
    select_n x1, other arithmetic, shards(): shifted = stiff - jnp.take(omega_sq, freq_idx)[None, :]  35.5 us
    unnamed x19, local copies, waits for them, and re-layouts  30 us
    scatter x2, other arithmetic, shards(): raw.at[:, :, iface_right].set(right_new).at[:, :, iface_left].set(left_new)  13.7 us
    reshape x2, local copies, waits for them, and re-layouts, shards(): (force - dev_rows[:, None, :] * response).reshape(local_sec, 2, width)  12.1 us
    dot_general x1, matrix products, shards(): jnp.einsum('skm,dm->skd', lax.all_gather(rounded, 'dof', axis=2, tiled=Tr...  10.3 us
    dot_general x1, matrix products, shards(): jnp.dot(loads.reshape(local_sec * rows_two, dof_rows), modes, preferred_e...  10.1 us
    all_to_all x1, starting transfers between devices, shards(): lax.all_to_all(rest, 'sector', split_axis=2, concat_axis=0, tiled=True)  8.35 us
  transfers between devices with their start and end apart: 5, of which 2 were waited for; matrix products, arithmetic and copies ran while one was open for 24% of the time, Pallas kernels for 0%

commit v1 on v0

--- a/solution.py
+++ b/solution.py
@@ -3,6 +3,13 @@
 import jax.numpy as jnp
 from jax import lax
 from jax.sharding import PartitionSpec as P
+
+
+def exchange_blocks(x, mesh_axis, split, join):
+    devices = lax.axis_size(mesh_axis)
+    tiles = jnp.stack(jnp.split(x, devices, axis=split), axis=0)
+    tiles = lax.all_to_all(tiles, mesh_axis, split_axis=0, concat_axis=0)
+    return jnp.concatenate(tiles, axis=join)
 
 
 def shifted_2(shard, axis, by):
@@ -76,12 +83,8 @@
     out_im = (
         jnp.dot(cosine, solved_im, precision=highest) + jnp.dot(sine, solved_re, precision=highest)
     ) / sectors
-    updated = lax.all_to_all(
-        jnp.stack([out_re, out_im], 1).astype(jnp.bfloat16),
-        "sector",
-        split_axis=0,
-        concat_axis=2,
-        tiled=True,
+    updated = exchange_blocks(
+        jnp.stack([out_re, out_im], 1).astype(jnp.bfloat16), "sector", 0, 2
     ).astype(jnp.float32)
     modal_response = updated.reshape(local_sec, rows_two, half)
     rounded = modal_response.astype(jnp.bfloat16)

time: 274 us -> 283 us (1.033)
  local copies, waits for them, and re-layouts: 74.7 us -> 83.6 us
    unnamed x19 -> x34, local copies, waits for them, and re-layouts: 30 us -> 39 us
  transfers between devices with their start and end apart: 5 -> 5, of which waited for: 2 -> 2; matrix products, arithmetic and copies ran while one was open for 24% -> 23% of each run, Pallas kernels for 0% -> 0%
where the time goes in v1:
time: 283 us; the launch traced here: 282 us
  other arithmetic  133 us (47%)
  local copies, waits for them, and re-layouts  83.6 us (30%)
  matrix products  23.1 us (8%)
  starting transfers between devices  17.6 us (6%)
  between operations  15.1 us (5%)
  waiting for transfers between devices  7.83 us (3%)
    unnamed x1, other arithmetic  74.5 us
    unnamed x34, local copies, waits for them, and re-layouts  39 us
    select_n x1, other arithmetic, shards(): shifted = stiff - jnp.take(omega_sq, freq_idx)[None, :]  35.5 us
    scatter x2, other arithmetic, shards(): raw.at[:, :, iface_right].set(right_new).at[:, :, iface_left].set(left_new)  13.7 us
    reshape x2, local copies, waits for them, and re-layouts, shards(): (force - dev_rows[:, None, :] * response).reshape(local_sec, 2, width)  12.1 us
    dot_general x1, matrix products, shards(): jnp.einsum('skm,dm->skd', lax.all_gather(rounded, 'dof', axis=2, tiled=Tr...  10.3 us
    dot_general x1, matrix products, shards(): jnp.dot(loads.reshape(local_sec * rows_two, dof_rows), modes, preferred_e...  10.1 us
    all_to_all x1, starting transfers between devices, shards(): lax.all_to_all(rest, 'sector', split_axis=2, concat_axis=0, tiled=True)  8.35 us
  transfers between devices with their start and end apart: 5, of which 2 were waited for; matrix products, arithmetic and copies ran while one was open for 23% of the time, Pallas kernels for 0%

profile of v1, /device:TPU:0, one launch (start us, length us, event | category | flops | bytes accessed | tf_op | source)
XLA Modules:
  0.0 282.0 jit_solution(8127292639535505862)
XLA Ops:
  7.3 10.1 %fusion.2 = f32[1,128,512]{2,1,0:T(8,128)} fusion(bf16[16384,512]{1,0:T(8,128)(2,1)} %param.13, bf16[1,128,16384]{2,1,0:T(8,128)(2,1)} %param.12), kind=kOutput, calls=%fused_computation.9 | convolution fusion | flops 2147483648 | bytes 21233664 | tf_op jit(solution)/shard_map/dot_general | solution.py:48
  19.0 0.7 fusion.105
  19.7 0.7 fusion.106
  20.4 0.7 fusion.103
  21.2 0.7 fusion.104
  22.6 6.9 %gather_fusion.1 = f32[1024]{0:T(1024)S(1)} fusion(f32[512]{0:T(512)S(1)} %copy-done.1, s32[1024]{0:T(1024)S(1)} %broadcast_clamp_fusion), kind=kCustom, calls=%fused_computation.3 | custom fusion | bytes 12288 | tf_op jit(solution)/shard_map/jit(_take)/gather | solution.py:71
  29.6 4.4 %compare_select_fusion.2 = f32[1024,1]{0,1:T(1,128)S(1)} fusion(f32[]{:T(128)} %bitcast.69, f32[]{:T(128)} %bitcast.70, f32[]{:T(128)} %bitcast.71, f32[]{:T(128)} %bitcast.72, f32[]{:T(128)} %bitcast.73, f32[]{:T(128)} %bitcast.75, f32[]{:T(128)} %bitcast.74, s32[]{:T(128)S(6)} %mul.129), kind=kLoop, calls=%fused_computation.152 | loop fusion | flops 31744 | bytes 4128 | tf_op jit(solution)/shard_map/jit(_take)/gather | solution.py:70
  34.1 0.9 multiply_subtract_fusion
  35.1 12.0 %copy.258 = f32[1,2,16384]{1,0,2:T(1,128)} copy(f32[1,2,16384]{2,1,0:T(2,128)S(1)} %reshape.262) | data formatting | bytes 262144 | tf_op jit(solution)/shard_map/reshape | solution.py:63
  47.1 0.5 broadcast.1041
  47.7 74.5 %reduce.114 = f32[16384,2]{1,0:T(8,128)} reduce(f32[16384,1,2]{2,1,0:T(1,128)} %bitcast.201, f32[]{:T(128)} %broadcast.1041), dimensions={1}, to_apply=%bitcast.184.reduce_sub_computation | reduce | bytes 262148
  122.1 8.2 %reshape.611 = f32[16,1,2048]{2,1,0:T(1,128)} reshape(f32[16384,2]{1,0:T(8,128)} %reduce.114) | data formatting | bytes 262144
  130.3 8.3 %all-to-all-start = ((f32[16,1,2048]{2,1,0:T(1,128)}), f32[16,1,2048]{2,1,0:T(1,128)S(1)}, u32[]{:S(2)}, u32[]{:S(2)}) async-start(f32[16,1,2048]{2,1,0:T(1,128)} %reshape.611), calls=%async_computation.1 | async-start | bytes 262144 | tf_op jit(solution)/shard_map/all_to_all | solution.py:64
  138.9 2.8 gather_fusion
  142.0 35.5 %select_select_fusion = f32[1024]{0:T(1024)S(1)} fusion(pred[1024]{0:T(1024)(128)(4,1)S(1)} %get-tuple-element.123, pred[1024]{0:T(1024)(128)(4,1)S(1)} %get-tuple-element.124, pred[1024]{0:T(1024)(128)(4,1)S(1)} %get-tuple-element.125, pred[1024]{0:T(1024)(128)(4,1)S(1)} %get-tuple-element.126, pred[1024]{0:T(1024)(128)(4,1)S(1)} %get-tuple-element.127, ...), kind=kLoop, calls=%fused_computation.202 | loop fusion | flops 81920 | bytes 66792 | tf_op jit(solution)/shard_map/jit(_take)/select_n | solution.py:70
  177.5 1.0 reduce.115
  178.5 14.7 %reshape.612 = f32[16384,1,2]{2,1,0:T(1,128)} reshape(f32[16,2048]{1,0:T(8,128)S(1)} %reduce.115) | data formatting | bytes 262144
  193.3 5.2 %copy.267 = f32[1,2,16,1024]{3,2,1,0:T(8,128)S(1)} copy(f32[1,2,16,1024]{1,3,2,0:T(8,128)} %bitcast.202) | data formatting | bytes 262144 | tf_op jit(solution)/shard_map/all_to_all | solution.py:64
  199.4 0.3 fusion.24
  201.2 0.6 constant_dynamic-update-slice_fusion.15
  201.8 0.6 constant_dynamic-update-slice_fusion.14
  202.4 0.6 constant_dynamic-update-slice_fusion.13
  203.0 0.6 constant_dynamic-update-slice_fusion.12
  203.6 0.6 constant_dynamic-update-slice_fusion.11
  204.2 0.6 constant_dynamic-update-slice_fusion.10
  204.8 0.6 constant_dynamic-update-slice_fusion.9
  205.4 0.6 constant_dynamic-update-slice_fusion.8
  206.0 0.6 constant_dynamic-update-slice_fusion.7
  206.6 0.6 constant_dynamic-update-slice_fusion.6
  207.2 0.6 constant_dynamic-update-slice_fusion.5
  207.8 0.6 constant_dynamic-update-slice_fusion.4
  208.4 0.6 constant_dynamic-update-slice_fusion.3
  209.0 0.6 constant_dynamic-update-slice_fusion.2
  209.6 0.6 constant_dynamic-update-slice_fusion.1
  210.2 0.6 constant_dynamic-update-slice_fusion
  210.8 6.9 %all-to-all-start.1 = ((bf16[16,1,2,1024]{3,2,1,0:T(2,128)(2,1)}), bf16[16,1,2,1024]{3,2,1,0:T(2,128)(2,1)S(1)}, u32[]{:S(2)}, u32[]{:S(2)}) async-start(bf16[16,1,2,1024]{3,2,1,0:T(2,128)(2,1)} %constant_dynamic-update-slice_fusion), calls=%async_computation.2 | async-start | bytes 131072 | tf_op jit(solution)/shard_map/all_to_all | solution.py:11
  217.7 7.5 %all-to-all-done.1 = bf16[16,1,2,1024]{3,2,1,0:T(2,128)(2,1)S(1)} async-done(((bf16[16,1,2,1024]{3,2,1,0:T(2,128)(2,1)}), bf16[16,1,2,1024]{3,2,1,0:T(2,128)(2,1)S(1)}, u32[]{:S(2)}, u32[]{:S(2)}) %all-to-all-start.1) | async-done | bytes 65568 | tf_op jit(solution)/shard_map/all_to_all | solution.py:11
  225.3 1.9 all_gather.3
  227.2 10.3 %convolution_convert_fusion = bf16[128,16384]{1,0:T(8,128)(2,1)} fusion(bf16[16384,512]{1,0:T(8,128)(2,1)} %param.13, bf16[1,128,512]{2,1,0:T(8,128)(2,1)S(1)} %all_gather.3), kind=kOutput, calls=%fused_computation.6 | convolution fusion | flops 2149580800 | bytes 21102592 | tf_op jit(solution)/shard_map/skm,dm->skd/dot_general | solution.py:91
  237.6 6.4 %copy.265 = bf16[128,16384]{0,1:T(8,128)(2,1)} copy(bf16[128,16384]{1,0:T(8,128)(2,1)} %convolution_convert_fusion) | data formatting | bytes 8388608 | tf_op jit(solution)/shard_map/convert_element_type | solution.py:96
  243.9 3.8 %gather_fusion.3 = bf16[512,128]{1,0:T(8,128)(2,1)S(1)} fusion(bf16[128,16384]{0,1:T(8,128)(2,1)} %copy.265, s32[1024]{0:T(1024)S(1)} %get-tuple-element.179), kind=kCustom, calls=%fused_computation.1.clone | custom fusion | bytes 264192 | tf_op jit(solution)/shard_map/jit(_take)/gather | solution.py:97
  247.9 1.0 collective-permute-start
  248.9 3.8 %gather_fusion.2 = bf16[512,128]{1,0:T(8,128)(2,1)S(1)} fusion(bf16[128,16384]{0,1:T(8,128)(2,1)} %copy.265, s32[1024]{0:T(1024)S(1)} %get-tuple-element.180), kind=kCustom, calls=%fused_computation.clone | custom fusion | bytes 264192 | tf_op jit(solution)/shard_map/jit(_take)/gather | solution.py:98
  252.8 1.3 collective-permute-start.1
  254.2 0.7 convert_element_type.61
  254.8 6.8 %scatter_custom_fusion = bf16[128,16384]{0,1:T(8,128)(2,1)} fusion(bf16[128,16384]{0,1:T(8,128)(2,1)} %copy.265, s32[512]{0:T(512)S(1)} %compare_select_fusion.14, bf16[1,128,512]{1,2,0:T(8,128)(2,1)S(1)} %collective-permute-done, f32[]{:T(128)} %constant.134.clone.1, bf16[512,128]{1,0:T(8,128)(2,1)S(1)} %gather_fusion.2, ...), kind=kCustom, calls=%fused_computation.53 | custom fusion | flops 393216 | bytes 4457472 | tf_op jit(solution)/shard_map/scatter | solution.py:109
  262.0 6.8 %scatter_custom_fusion.1 = bf16[128,16384]{0,1:T(8,128)(2,1)} fusion(bf16[128,16384]{0,1:T(8,128)(2,1)} %scatter_custom_fusion, s32[512]{0:T(512)S(1)} %compare_select_fusion.13, bf16[1,128,512]{1,2,0:T(8,128)(2,1)S(1)} %collective-permute-done.1, f32[]{:T(128)} %constant.134.clone.1, bf16[512,128]{1,0:T(8,128)(2,1)S(1)} %gather_fusion.3, ...), kind=kCustom, calls=%fused_computation.55 | custom fusion | flops 393216 | bytes 4457472 | tf_op jit(solution)/shard_map/scatter | solution.py:109
  268.8 6.4 %copy.266 = bf16[1,128,16384]{2,1,0:T(8,128)(2,1)} copy(bf16[1,128,16384]{1,2,0:T(8,128)(2,1)} %bitcast.203) | data formatting | bytes 8388608
  (76 shorter events, 5.4 us)
Async XLA Ops:
  7.2 22.3 %copy-start = (f32[8,512]{1,0:T(8,128)S(1)}, f32[8,512]{1,0:T(8,128)}, u32[]{:S(2)}) copy-start(f32[8,512]{1,0:T(8,128)} %param.16) | copy-start | bytes 49156
  7.2 11.8 %copy-start.2 = (f32[64]{0:T(128)S(1)}, f32[64]{0:T(128)}, u32[]{:S(2)}) copy-start(f32[64]{0:T(128)} %param.19) | copy-start | bytes 772
  7.2 14.7 %copy-start.5 = (s32[512]{0:T(512)S(1)}, s32[512]{0:T(512)}, u32[]{:S(2)}) copy-start(s32[512]{0:T(512)} %param.20) | copy-start | bytes 6148
  7.2 15.4 %copy-start.1 = (f32[512]{0:T(512)S(1)}, f32[512]{0:T(512)}, u32[]{:S(2)}) copy-start(f32[512]{0:T(512)} %param.18) | copy-start | bytes 6148
  7.2 26.9 %reduce-scatter.2.cloned.1.call-start = ((), (), s32[]{:S(2)}) async-start(), calls=%async_computation.3 | async-start | bytes 393216 | tf_op jit(solution)/shard_map/reduce_scatter | solution.py:51
  17.4 16.7 %copy-start.6 = (s32[512]{0:T(512)S(1)}, s32[512]{0:T(512)}, u32[]{:S(2)}) copy-start(s32[512]{0:T(512)} %param.21) | copy-start | bytes 6148
  17.4 16.7 %copy-start.3 = (f32[1,128,256]{2,1,0:T(8,128)S(1)}, f32[1,128,256]{2,1,0:T(8,128)}, u32[]{:S(2)}) copy-start(f32[1,128,256]{2,1,0:T(8,128)} %param.14) | copy-start | bytes 393220
  122.1 16.6 %copy-start.4 = (f32[16,512]{1,0:T(8,128)S(1)}, f32[16,512]{1,0:T(8,128)}, u32[]{:S(2)}) copy-start(f32[16,512]{1,0:T(8,128)} %param.17) | copy-start | bytes 98308
  130.3 47.2 %all-to-all-start = ((f32[16,1,2048]{2,1,0:T(1,128)}), f32[16,1,2048]{2,1,0:T(1,128)S(1)}, u32[]{:S(2)}, u32[]{:S(2)}) async-start(f32[16,1,2048]{2,1,0:T(1,128)} %reshape.611), calls=%async_computation.1 | async-start | bytes 262144 | tf_op jit(solution)/shard_map/all_to_all | solution.py:64
  210.8 14.4 %all-to-all-start.1 = ((bf16[16,1,2,1024]{3,2,1,0:T(2,128)(2,1)}), bf16[16,1,2,1024]{3,2,1,0:T(2,128)(2,1)S(1)}, u32[]{:S(2)}, u32[]{:S(2)}) async-start(bf16[16,1,2,1024]{3,2,1,0:T(2,128)(2,1)} %constant_dynamic-update-slice_fusion), calls=%async_computation.2 | async-start | bytes 131072 | tf_op jit(solution)/shard_map/all_to_all | solution.py:11
  247.9 7.0 %collective-permute-start = (bf16[1,128,512]{1,2,0:T(8,128)(2,1)S(1)}, bf16[1,128,512]{1,2,0:T(8,128)(2,1)S(1)}, u32[]{:S(2)}, u32[]{:S(2)}) collective-permute-start(bf16[1,128,512]{1,2,0:T(8,128)(2,1)S(1)} %bitcast_select_fusion), channel_id=1, source_target_pairs={{0,30},{2,0},{4,2},{6,4},{8,6},{10,8},{12,10},{14,12},{16,14},{18,... | collective-permute-start | bytes 393224 | tf_op jit(solution)/shard_map/ppermute | solution.py:17
  252.8 9.1 %collective-permute-start.1 = (bf16[1,128,512]{1,2,0:T(8,128)(2,1)S(1)}, bf16[1,128,512]{1,2,0:T(8,128)(2,1)S(1)}, u32[]{:S(2)}, u32[]{:S(2)}) collective-permute-start(bf16[1,128,512]{1,2,0:T(8,128)(2,1)S(1)} %bitcast_select_fusion.1), channel_id=1, source_target_pairs={{0,2},{2,4},{4,6},{6,8},{8,10},{10,12},{12,14},{14,16},{16,18},{18... | collective-permute-start | bytes 393224 | tf_op jit(solution)/shard_map/ppermute | solution.py:17
Sparse Core Ops, SparseCore 0:
  17.5 10.4 reduce-scatter.1
